TPU v7x, 32 devices: a whole 2x2x4 slice. The times are simulated.
32 devices in a mesh: wide: 2 (over core), op: 16 (over z, y, x).
Axes of the slice: x: 2, y: 2, z: 4, core: 2. Of those that a mesh axis runs over, the one named last changes fastest.
Arguments:
- wavefunction: bfloat16 [32, 4, 512, 512], P('wide', None, 'op'), may hold values from -6 to 6
- left_ops: bfloat16 [128, 512, 512], P(('wide', 'op')), may hold values from -0.0390625 to 0.0390625
- right_ops: bfloat16 [128, 512, 512], P(('wide', 'op')), may hold values from -0.25 to 0.25
- in_sector: int32 [128], P(('wide', 'op')), may hold values from 0 to 31
- live_count: int32 [32], P(('wide', 'op')), may hold values from 2 to 4, as said below
Outputs:
- sigma_blocks: bfloat16 [2, 4, 512, 512], P('wide', None, 'op')
Inputs may be any that keep to these rules, and one draw needn't show every extreme that they name: `live_count`: in each aligned group of 16 entries (the devices of one op group), entries i and i + 8 sum to 6, and exactly 4 entries are 4.
All inputs are finite; a program needn't handle non-finite values.
Results may differ from a plain program's by a relative error of at most 0.0065.
Values may be sent and summed in bfloat16 or wider, within the bound.
A program may use at most 64 MiB of HBM per device.

v0:
```python
import jax
import jax.numpy as jnp
from jax import lax
from jax.sharding import PartitionSpec as P


def from_behind(x, axis, by):
    devices = lax.axis_size(axis)
    return lax.ppermute(x, axis, [(i, (i + by) % devices) for i in range(devices)])


def sandwich(sector, left_op, right_op):
    half_step = jnp.einsum(
        "smk,nk->smn", sector, right_op, preferred_element_type=jnp.float32
    ).astype(jnp.bfloat16)
    return jnp.einsum("im,smn->sin", left_op, half_step, preferred_element_type=jnp.float32)


def local(wavefunction, left_ops, right_ops, in_sector, live_count):
    group_size = lax.axis_size("op")
    slot_count = left_ops.shape[0]
    ins_all, live_all = (
        lax.all_gather(in_sector, "op", axis=0, tiled=True),
        lax.all_gather(live_count, "op", axis=0, tiled=True),
    )
    ins_grid = ins_all.reshape(group_size, slot_count)
    my_live = live_count[0]
    rows_all = lax.all_gather(wavefunction, "wide", axis=0, tiled=True)
    partner_ins = jnp.roll(ins_grid[:, slot_count - 1], group_size // 2)
    third_in = jnp.where(live_all >= 3, ins_grid[:, 2], partner_ins)
    work_grid = jnp.concatenate([ins_grid[:, :2], third_in[:, None]], axis=1)
    arrived_left, arrived_right = from_behind(
        (left_ops[slot_count - 1], right_ops[slot_count - 1]), "op", group_size // 2
    )
    own_third = my_live >= 3
    work_left = jnp.stack(
        [left_ops[0], left_ops[1], jnp.where(own_third, left_ops[2], arrived_left)]
    )
    work_right = jnp.stack(
        [right_ops[0], right_ops[1], jnp.where(own_third, right_ops[2], arrived_right)]
    )
    weights = [jnp.float32(1.0) for slot_index in range(slot_count - 1)]
    work_count = work_grid.shape[1]
    outgoing = jnp.take(rows_all, work_grid.reshape(-1), axis=0)
    arrived = lax.all_to_all(outgoing, "op", split_axis=0, concat_axis=2, tiled=True)
    partial_value = jnp.zeros(arrived.shape[1:], jnp.float32)
    for slot_index in range(work_count):
        partial_value = partial_value + weights[slot_index] * sandwich(
            arrived[slot_index], work_left[slot_index], work_right[slot_index]
        )
    summed = lax.psum_scatter(partial_value[None], "op", scatter_dimension=2, tiled=True)
    return summed.astype(jnp.bfloat16)


def solution(mesh):
    placed = (
        P("wide", None, "op", None),
        P(("wide", "op"), None, None),
        P(("wide", "op"), None, None),
        P(("wide", "op")),
        P(("wide", "op")),
    )
    return jax.shard_map(
        local, mesh=mesh, in_specs=placed, out_specs=P("wide", None, "op", None), check_vma=False
    )
```

profile of v0, /device:TPU:0, one launch (start us, length us, event | category | flops | bytes accessed | tf_op | source)
XLA Modules:
  0.0 432.0 jit_solution(4435426553336007252)
XLA Ops:
  6.5 0.7 all-gather.2.cloned.1.call-update
  7.9 0.6 fusion.34
  9.2 0.7 dynamic-update-slice.1
  10.1 16.2 %all-reduce.3 = (s32[64]{0:T(128)S(1)}, s32[16]{0:T(128)S(1)}) all-reduce(s32[64]{0:T(128)S(1)} %dynamic-update-slice, s32[16]{0:T(128)S(1)} %dynamic-update-slice.1), channel_id=1, replica_groups=mesh['wide'=2,'op'=16] {'op'}, use_global_device_ids=true, to_apply=%add | all-reduce | flops 80 | bytes 640
  27.3 7.1 %gather_fusion = bf16[48,4,32,512]{3,2,1,0:T(8,128)(2,1)} fusion(bf16[32,4,32,512]{3,2,1,0:T(8,128)(2,1)} %all-gather.2.cloned.1.call-done, s32[1024]{0:T(1024)S(1)} %pad_clamp_fusion), kind=kCustom, calls=%fused_computation | custom fusion | bytes 12583104 | tf_op jit(solution)/shard_map/jit(_take)/gather | solution.py:44
  34.5 6.1 %broadcast_select_fusion = bf16[48,4,32,512]{3,2,1,0:T(8,128)(2,1)} fusion(bf16[48,4,32,512]{3,2,1,0:T(8,128)(2,1)} %gather_fusion, pred[48]{0:T(512)(128)(4,1)S(1)} %compare_and_fusion), kind=kLoop, calls=%fused_computation.1 | loop fusion | flops 3145728 | bytes 12582960 | tf_op jit(solution)/shard_map/jit(_take)/select_n | solution.py:44
  40.6 4.8 %all-to-all-start = ((bf16[48,4,32,512]{3,2,1,0:T(8,128)(2,1)}), bf16[48,4,32,512]{3,2,1,0:T(8,128)(2,1)}, u32[]{:S(2)}, u32[]{:S(2)}) async-start(bf16[48,4,32,512]{3,2,1,0:T(8,128)(2,1)} %broadcast_select_fusion), calls=%async_computation | async-start | bytes 12582912 | tf_op jit(solution)/shard_map/all_to_all | solution.py:45
  45.4 1.9 slice_bitcast_fusion.1
  47.3 2.8 collective-permute-start
  50.1 1.9 slice_bitcast_fusion
  52.8 134.8 %all-to-all-done = bf16[48,4,32,512]{3,2,1,0:T(8,128)(2,1)} async-done(((bf16[48,4,32,512]{3,2,1,0:T(8,128)(2,1)}), bf16[48,4,32,512]{3,2,1,0:T(8,128)(2,1)}, u32[]{:S(2)}, u32[]{:S(2)}) %all-to-all-start) | async-done | bytes 6291488 | tf_op jit(solution)/shard_map/all_to_all | solution.py:45
  187.7 5.1 %fusion.33 = (bf16[1,4,16,32,512]{4,3,1,0,2:T(8,128)(2,1)}, bf16[1,4,16,32,512]{4,3,1,0,2:T(8,128)(2,1)S(1)}, bf16[1,4,16,32,512]{4,3,1,0,2:T(8,128)(2,1)S(1)}) fusion(bf16[3,4,16,32,512]{4,3,1,0,2:T(8,128)(2,1)} %bitcast.5), kind=kLoop, calls=%fused_computation.40 | loop fusion | bytes 12582912 | tf_op jit(solution)/shard_map/slice | solution.py:49
  192.8 1.6 copy.32
  194.4 6.1 %fusion.1 = f32[4,512,512]{2,1,0:T(8,128)} fusion(bf16[4,512,512]{2,1,0:T(8,128)(2,1)} %bitcast.64, bf16[4,512,512]{2,1,0:T(8,128)(2,1)} %param.6, bf16[4,512,512]{2,1,0:T(8,128)(2,1)} %param.7), kind=kOutput, calls=%fused_computation.4 | convolution fusion | flops 2148532224 | bytes 7340032 | tf_op jit(solution)/shard_map/im,smn->sin/dot_general | solution.py:16
  200.5 1.5 copy.30
  202.0 0.8 copy-done
  202.9 0.2 copy.34
  203.1 6.2 %fusion.3 = f32[4,512,512]{2,1,0:T(8,128)} fusion(bf16[4,512,512]{2,1,0:T(8,128)(2,1)} %bitcast.63, bf16[4,512,512]{2,1,0:T(8,128)(2,1)} %param.6, bf16[4,512,512]{2,1,0:T(8,128)(2,1)} %param.7), kind=kOutput, calls=%fused_computation.6 | convolution fusion | flops 2148532224 | bytes 7340032 | tf_op jit(solution)/shard_map/im,smn->sin/dot_general | solution.py:16
  209.3 9.3 %collective-permute-done = bf16[512,512]{1,0:T(8,128)(2,1)S(1)} collective-permute-done((bf16[512,512]{1,0:T(8,128)(2,1)}, bf16[512,512]{1,0:T(8,128)(2,1)S(1)}, u32[]{:S(2)}, u32[]{:S(2)}) %collective-permute-start) | collective-permute-done | bytes 524320 | tf_op jit(solution)/shard_map/ppermute | solution.py:9
  218.5 10.3 %collective-permute-done.1 = bf16[512,512]{1,0:T(8,128)(2,1)S(1)} collective-permute-done((bf16[512,512]{1,0:T(8,128)(2,1)}, bf16[512,512]{1,0:T(8,128)(2,1)S(1)}, u32[]{:S(2)}, u32[]{:S(2)}) %collective-permute-start.1) | collective-permute-done | bytes 524320 | tf_op jit(solution)/shard_map/ppermute | solution.py:9
  228.8 8.2 %add_bitcast_fusion = f32[1,4,512,512]{2,3,1,0:T(8,128)} fusion(f32[4,512,512]{2,1,0:T(8,128)} %fusion.3, f32[4,512,512]{2,1,0:T(8,128)} %fusion.1, bf16[4,512,512]{2,1,0:T(8,128)(2,1)S(1)} %bitcast.62, bf16[512,512]{1,0:T(8,128)(2,1)S(1)} %collective-permute-done.1, bf16[512,512]{1,0:T(8,128)(2,1)S(1)} %collective-permute-done, ...), kind=kOutput, calls=%fused_computation.2 | convolution fusion | flops 2151153664 | bytes 16778240 | tf_op jit(solution)/shard_map/im,smn->sin/dot_general | solution.py:16
  237.0 5.4 %copy.36 = f32[1,4,512,512]{3,1,0,2:T(4,128)} copy(f32[1,4,512,512]{2,3,1,0:T(8,128)} %add_bitcast_fusion) | data formatting | bytes 8388608 | tf_op jit(solution)/shard_map/broadcast_in_dim | solution.py:51
  242.4 182.0 %all-reduce.5 = bf16[1,4,512,512]{3,1,0,2:T(4,128)(2,1)S(1)} all-reduce(f32[1,4,512,512]{3,1,0,2:T(4,128)} %copy.36), channel_id=2, replica_groups=mesh['wide'=2,'op'=16] {'op'}, use_global_device_ids=true, to_apply=%region_0.1.clone | all-reduce | flops 1048576 | bytes 6291456
  424.5 0.7 copy.37
  (23 shorter events, 1.4 us)
Async XLA Ops:
  6.5 1.4 copy-start.1
  6.5 3.3 copy-start.2
  6.5 20.8 %all-gather.2.cloned.1.call-start = ((), (), s32[]{:S(2)}) async-start(), calls=%async_computation.1 | async-start | bytes 6291456 | tf_op jit(solution)/shard_map/all_gather | solution.py:28
  40.6 147.1 %all-to-all-start = ((bf16[48,4,32,512]{3,2,1,0:T(8,128)(2,1)}), bf16[48,4,32,512]{3,2,1,0:T(8,128)(2,1)}, u32[]{:S(2)}, u32[]{:S(2)}) async-start(bf16[48,4,32,512]{3,2,1,0:T(8,128)(2,1)} %broadcast_select_fusion), calls=%async_computation | async-start | bytes 12582912 | tf_op jit(solution)/shard_map/all_to_all | solution.py:45
  47.3 171.2 %collective-permute-start = (bf16[512,512]{1,0:T(8,128)(2,1)}, bf16[512,512]{1,0:T(8,128)(2,1)S(1)}, u32[]{:S(2)}, u32[]{:S(2)}) collective-permute-start(bf16[512,512]{1,0:T(8,128)(2,1)} %slice_bitcast_fusion.1), channel_id=1, source_target_pairs={{0,8},{1,9},{2,10},{3,11},{4,12},{5,13},{6,14},{7,15},{8,0},{9,1},... | collective-permute-start | bytes 1572872 | tf_op jit(solution)/shard_map/ppermute | solution.py:9
  52.0 176.8 %collective-permute-start.1 = (bf16[512,512]{1,0:T(8,128)(2,1)}, bf16[512,512]{1,0:T(8,128)(2,1)S(1)}, u32[]{:S(2)}, u32[]{:S(2)}) collective-permute-start(bf16[512,512]{1,0:T(8,128)(2,1)} %slice_bitcast_fusion), channel_id=1, source_target_pairs={{0,8},{1,9},{2,10},{3,11},{4,12},{5,13},{6,14},{7,15},{8,0},{9,1},... | collective-permute-start | bytes 1572872 | tf_op jit(solution)/shard_map/ppermute | solution.py:9
  200.5 2.3 copy-start
Sparse Core Ops, SparseCore 0:
  8.9 16.3 all-gather.1
where the time goes:
time: 433 us; the launch traced here: 432 us
  blocking collectives  198 us (46%)
  waiting for transfers between devices  155 us (36%)
  local copies, waits for them, and re-layouts  28.8 us (7%)
  matrix products  20.5 us (5%)
  between operations  15.4 us (4%)
  starting transfers between devices  7.76 us (2%)
  other arithmetic  6.28 us (1%)
    unnamed x2, blocking collectives  198 us
    all_to_all x1, waiting for transfers between devices, local(): lax.all_to_all(outgoing, 'op', split_axis=0, concat_axis=2, tiled=True)  135 us
    dot_general x3, matrix products, sandwich(): jnp.einsum('im,smn->sin', left_op, half_step, preferred_element_type=jnp....  20.5 us
    ppermute x2, waiting for transfers between devices, from_behind(): lax.ppermute(x, axis, [(i, (i + by) % devices) for i in range(devices)])  19.5 us
  transfers between devices with their start and end apart: 4, of which 3 were waited for; matrix products, arithmetic and copies ran while one was open for 6% of the time, Pallas kernels for 0%

commit v1 on v0

--- a/solution.py
+++ b/solution.py
@@ -42,7 +42,10 @@
     weights = [jnp.float32(1.0) for slot_index in range(slot_count - 1)]
     work_count = work_grid.shape[1]
     outgoing = jnp.take(rows_all, work_grid.reshape(-1), axis=0)
-    arrived = lax.all_to_all(outgoing, "op", split_axis=0, concat_axis=2, tiled=True)
+    arrived = jnp.concatenate(
+        lax.all_to_all(jnp.stack(jnp.split(outgoing, lax.axis_size("op"), axis=0)), "op", 0, 0),
+        axis=2,
+    )
     partial_value = jnp.zeros(arrived.shape[1:], jnp.float32)
     for slot_index in range(work_count):
         partial_value = partial_value + weights[slot_index] * sandwich(

time: 433 us -> 441 us (1.018)
  local copies, waits for them, and re-layouts: 28.8 us -> 40 us
    unnamed x11 -> x20, local copies, waits for them, and re-layouts: 2.38 us -> 14.9 us
    slice x4 -> x1, local copies, waits for them, and re-layouts: 8.5 us -> 2.83 us  [local(): arrived[slot_index]]
    ppermute x2, waiting for transfers between devices: 19.5 us -> 24.8 us  [from_behind(): lax.ppermute(x, axis, [(i, (i + by) % devices) for i in range(devices)])]
where the time goes in v1:
time: 441 us; the launch traced here: 440 us
  blocking collectives  196 us (44%)
  waiting for transfers between devices  157 us (36%)
  local copies, waits for them, and re-layouts  40 us (9%)
  matrix products  20.5 us (5%)
  between operations  15.5 us (4%)
  starting transfers between devices  7.73 us (2%)
    unnamed x2, blocking collectives  196 us
    all_to_all x1, waiting for transfers between devices, local(): lax.all_to_all(jnp.stack(jnp.split(outgoing, lax.axis_size('op'), axis=0)...  131 us
    ppermute x2, waiting for transfers between devices, from_behind(): lax.ppermute(x, axis, [(i, (i + by) % devices) for i in range(devices)])  24.8 us
    dot_general x3, matrix products, sandwich(): jnp.einsum('im,smn->sin', left_op, half_step, preferred_element_type=jnp....  20.5 us
    unnamed x20, local copies, waits for them, and re-layouts  14.9 us
  transfers between devices with their start and end apart: 4, of which 3 were waited for; matrix products, arithmetic and copies ran while one was open for 6% of the time, Pallas kernels for 0%

profile of v1, /device:TPU:0, one launch (start us, length us, event | category | flops | bytes accessed | tf_op | source)
XLA Modules:
  0.0 439.9 jit_solution(6822524393503768499)
XLA Ops:
  7.9 1.4 fusion.50
  10.0 0.8 dynamic-update-slice.1
  10.8 0.8 dynamic-update-slice
  11.7 16.2 %all-reduce.3 = (s32[64]{0:T(128)S(1)}, s32[16]{0:T(128)S(1)}) all-reduce(s32[64]{0:T(128)S(1)} %dynamic-update-slice, s32[16]{0:T(128)S(1)} %dynamic-update-slice.1), channel_id=1, replica_groups=mesh['wide'=2,'op'=16] {'op'}, use_global_device_ids=true, to_apply=%add | all-reduce | flops 80 | bytes 640
  28.8 7.2 %gather_fusion = bf16[48,4,32,512]{3,2,1,0:T(8,128)(2,1)} fusion(bf16[32,4,32,512]{3,2,1,0:T(8,128)(2,1)} %all-gather.2.cloned.1.call-done, s32[1024]{0:T(1024)S(1)} %pad_clamp_fusion), kind=kCustom, calls=%fused_computation | custom fusion | bytes 12583104 | tf_op jit(solution)/shard_map/jit(_take)/gather | solution.py:44
  36.0 3.4 broadcast_select_fusion
  39.5 0.8 fusion.46
  43.4 0.8 fusion.41
  45.0 0.8 fusion.39
  48.2 0.8 fusion.35
  52.1 4.8 %all-to-all-start = ((bf16[16,3,4,32,512]{4,3,2,1,0:T(8,128)(2,1)}), bf16[16,3,4,32,512]{4,3,2,1,0:T(8,128)(2,1)}, u32[]{:S(2)}, u32[]{:S(2)}) async-start(bf16[16,3,4,32,512]{4,3,2,1,0:T(8,128)(2,1)} %fusion.31), calls=%async_computation | async-start | bytes 12582912 | tf_op jit(solution)/shard_map/all_to_all | solution.py:46
  57.0 1.9 slice_bitcast_fusion.1
  58.9 2.5 collective-permute-start
  61.4 1.9 slice_bitcast_fusion
  64.4 131.0 %all-to-all-done = bf16[16,3,4,32,512]{4,3,2,1,0:T(8,128)(2,1)} async-done(((bf16[16,3,4,32,512]{4,3,2,1,0:T(8,128)(2,1)}), bf16[16,3,4,32,512]{4,3,2,1,0:T(8,128)(2,1)}, u32[]{:S(2)}, u32[]{:S(2)}) %all-to-all-start) | async-done | bytes 6291488 | tf_op jit(solution)/shard_map/all_to_all | solution.py:46
  195.4 3.6 copy.45
  198.9 2.8 fusion.49
  201.8 6.1 %fusion.1 = f32[4,512,512]{2,1,0:T(8,128)} fusion(bf16[4,512,512]{2,1,0:T(8,128)(2,1)} %bitcast.129, bf16[4,512,512]{2,1,0:T(8,128)(2,1)} %param.6, bf16[4,512,512]{2,1,0:T(8,128)(2,1)} %param.7), kind=kOutput, calls=%fused_computation.5 | convolution fusion | flops 2148532224 | bytes 7340032 | tf_op jit(solution)/shard_map/im,smn->sin/dot_general | solution.py:16
  207.9 6.2 %fusion.3 = f32[4,512,512]{2,1,0:T(8,128)} fusion(bf16[4,512,512]{2,1,0:T(8,128)(2,1)} %bitcast.128, bf16[4,512,512]{2,1,0:T(8,128)(2,1)} %param.6, bf16[4,512,512]{2,1,0:T(8,128)(2,1)} %param.7), kind=kOutput, calls=%fused_computation.7 | convolution fusion | flops 2148532224 | bytes 7340032 | tf_op jit(solution)/shard_map/im,smn->sin/dot_general | solution.py:16
  214.1 14.6 %collective-permute-done = bf16[512,512]{1,0:T(8,128)(2,1)S(1)} collective-permute-done((bf16[512,512]{1,0:T(8,128)(2,1)}, bf16[512,512]{1,0:T(8,128)(2,1)S(1)}, u32[]{:S(2)}, u32[]{:S(2)}) %collective-permute-start) | collective-permute-done | bytes 524320 | tf_op jit(solution)/shard_map/ppermute | solution.py:9
  228.6 10.2 %collective-permute-done.1 = bf16[512,512]{1,0:T(8,128)(2,1)S(1)} collective-permute-done((bf16[512,512]{1,0:T(8,128)(2,1)}, bf16[512,512]{1,0:T(8,128)(2,1)S(1)}, u32[]{:S(2)}, u32[]{:S(2)}) %collective-permute-start.1) | collective-permute-done | bytes 524320 | tf_op jit(solution)/shard_map/ppermute | solution.py:9
  238.9 8.2 %add_bitcast_fusion = f32[1,4,512,512]{2,3,1,0:T(8,128)} fusion(f32[4,512,512]{2,1,0:T(8,128)} %fusion.3, f32[4,512,512]{2,1,0:T(8,128)} %fusion.1, bf16[4,512,512]{2,1,0:T(8,128)(2,1)S(1)} %bitcast.127, bf16[512,512]{1,0:T(8,128)(2,1)S(1)} %collective-permute-done.1, bf16[512,512]{1,0:T(8,128)(2,1)S(1)} %collective-permute-done, ...), kind=kOutput, calls=%fused_computation.3 | convolution fusion | flops 2151153664 | bytes 16778240 | tf_op jit(solution)/shard_map/im,smn->sin/dot_general | solution.py:16
  247.0 5.4 %copy.39 = f32[1,4,512,512]{3,1,0,2:T(4,128)} copy(f32[1,4,512,512]{2,3,1,0:T(8,128)} %add_bitcast_fusion) | data formatting | bytes 8388608 | tf_op jit(solution)/shard_map/broadcast_in_dim | solution.py:54
  252.5 179.8 %all-reduce.5 = bf16[1,4,512,512]{3,1,0,2:T(4,128)(2,1)S(1)} all-reduce(f32[1,4,512,512]{3,1,0,2:T(4,128)} %copy.39), channel_id=2, replica_groups=mesh['wide'=2,'op'=16] {'op'}, use_global_device_ids=true, to_apply=%region_0.1.clone | all-reduce | flops 1048576 | bytes 6291456
  (31 shorter events, 12.2 us)
Async XLA Ops:
  6.5 22.3 %all-gather.2.cloned.1.call-start = ((), (), s32[]{:S(2)}) async-start(), calls=%async_computation.1 | async-start | bytes 6291456 | tf_op jit(solution)/shard_map/all_gather | solution.py:28
  52.1 143.2 %all-to-all-start = ((bf16[16,3,4,32,512]{4,3,2,1,0:T(8,128)(2,1)}), bf16[16,3,4,32,512]{4,3,2,1,0:T(8,128)(2,1)}, u32[]{:S(2)}, u32[]{:S(2)}) async-start(bf16[16,3,4,32,512]{4,3,2,1,0:T(8,128)(2,1)} %fusion.31), calls=%async_computation | async-start | bytes 12582912 | tf_op jit(solution)/shard_map/all_to_all | solution.py:46
  58.9 169.7 %collective-permute-start = (bf16[512,512]{1,0:T(8,128)(2,1)}, bf16[512,512]{1,0:T(8,128)(2,1)S(1)}, u32[]{:S(2)}, u32[]{:S(2)}) collective-permute-start(bf16[512,512]{1,0:T(8,128)(2,1)} %slice_bitcast_fusion.1), channel_id=1, source_target_pairs={{0,8},{1,9},{2,10},{3,11},{4,12},{5,13},{6,14},{7,15},{8,0},{9,1},... | collective-permute-start | bytes 1572872 | tf_op jit(solution)/shard_map/ppermute | solution.py:9
  63.3 175.6 %collective-permute-start.1 = (bf16[512,512]{1,0:T(8,128)(2,1)}, bf16[512,512]{1,0:T(8,128)(2,1)S(1)}, u32[]{:S(2)}, u32[]{:S(2)}) collective-permute-start(bf16[512,512]{1,0:T(8,128)(2,1)} %slice_bitcast_fusion), channel_id=1, source_target_pairs={{0,8},{1,9},{2,10},{3,11},{4,12},{5,13},{6,14},{7,15},{8,0},{9,1},... | collective-permute-start | bytes 1572872 | tf_op jit(solution)/shard_map/ppermute | solution.py:9
Sparse Core Ops, SparseCore 0:
  8.9 16.3 all-gather.1
